TPU v7x, 512 devices: a whole 4x4x16 slice. The times are simulated.
512 devices in a mesh: tm: 4 (over z_hi, core), height: 16 (over x, y), panel: 8 (over z_lo).
Axes of the slice: x: 4, y: 4, z: 16 (z_hi: 2, z_lo: 8; z = z_hi * 8 + z_lo), core: 2. Of those that a mesh axis runs over, the one named last changes fastest.
Arguments:
- activations: bfloat16 [6, 8, 32, 512, 128], P(None, 'tm', 'height', 'panel'), may hold values from -6 to 6
- out_grad: bfloat16 [6, 8, 32, 512, 128], P(None, 'tm', 'height'), may hold values from -0.019042969 to 0.019042969
- out_basis: bfloat16 [512, 512], replicated, may hold values from -0.25 to 0.25
- in_basis: bfloat16 [13824, 13824], P('panel', ('tm', 'height')), may hold values from -0.0546875 to 0.0546875
- eigenvalues: float32 [512, 13824], P('panel', ('tm', 'height')), may hold values from 0.05 to 5
- forget_order: int32 [6], replicated, may hold values from 0 to 5, each once
Outputs:
- correction: float32 [512, 13824], P('panel', ('tm', 'height'))
Inputs may be any that keep to these rules, and one draw needn't show every extreme that they name: `forget_order`: a permutation of the clip ids.
All inputs are finite; a program needn't handle non-finite values.
Results may differ from a plain program's by a relative error of at most 0.0041.
Values may be sent and summed in bfloat16 or wider, within the bound.
A program may use at most 64 MiB of HBM per device.

v0:
```python
import jax
import jax.numpy as jnp
from jax import lax
from jax.sharding import PartitionSpec as P

FORGET = 3


damping = 0.1


def from_behind(value, axis, steps):
    count = lax.axis_size(axis)
    leading, last = (max(0, -steps), min(count, count - steps))
    return lax.ppermute(value, axis, [(source, source + steps) for source in range(leading, last)])


def with_halo(block, sides, width):
    for axis, dim in sides:
        count = lax.axis_size(axis)
        forward = [(i, i + 1) for i in range(count - 1)]
        backward = [(target, source) for source, target in forward]
        low = lax.ppermute(
            lax.slice_in_dim(block, block.shape[dim] - width, None, axis=dim), axis, forward
        )
        high = lax.ppermute(lax.slice_in_dim(block, 0, width, axis=dim), axis, backward)
        block = jnp.concatenate([low, block, high], axis=dim)
    return block


def body(activations, out_grad, out_basis, in_basis, eigenvalues, forget_order):
    chosen = forget_order[:FORGET]
    sel_act = jnp.take(activations, chosen, axis=0)
    sel_grad = jnp.take(out_grad, chosen, axis=0)
    frames = sel_act.shape[1]
    rows = sel_act.shape[2]
    channels = sel_act.shape[3]
    wide = sel_act.shape[4]
    outputs = sel_grad.shape[3]
    projected = jnp.einsum(
        "nfrow,ok->nfrkw", sel_grad, out_basis, preferred_element_type=jnp.float32
    ).astype(jnp.bfloat16)
    previous = from_behind(sel_act, "tm", 1)
    extended = jnp.concatenate([previous, sel_act], axis=1)
    rimmed = with_halo(extended, (("height", 2),), 1)
    padded = jnp.pad(rimmed, ((0, 0), (0, 0), (0, 0), (0, 0), (1, 1)))
    windows = []
    for shift_t in range(3):
        for shift_h in range(3):
            for shift_w in range(3):
                windows.append(
                    padded[
                        :,
                        shift_t : shift_t + frames,
                        shift_h : shift_h + rows,
                        :,
                        shift_w : shift_w + wide,
                    ]
                )
    stacked = jnp.stack(windows, axis=0)
    partial_grad = jnp.einsum(
        "nfrkw,tnfrcw->kct", projected, stacked, preferred_element_type=jnp.float32
    )
    partial_grad = partial_grad.reshape(outputs, channels * 27)
    summed = lax.psum(partial_grad, ("tm", "height"))
    grad = summed.astype(jnp.bfloat16)
    rotated = jnp.dot(grad, in_basis, preferred_element_type=jnp.float32)
    reduced = lax.psum_scatter(rotated, "panel", scatter_dimension=0, tiled=True)
    return reduced / (eigenvalues + damping)


def solution(mesh):
    in_specs = (
        P(None, "tm", "height", "panel", None),
        P(None, "tm", "height", None, None),
        P(),
        P("panel", ("tm", "height")),
        P("panel", ("tm", "height")),
        P(),
    )
    out_specs = P("panel", ("tm", "height"))
    return jax.shard_map(body, mesh=mesh, in_specs=in_specs, out_specs=out_specs, check_vma=False)
```

profile of v0, /device:TPU:1, one launch (start us, length us, event | category | flops | bytes accessed | tf_op | source)
XLA Modules:
  0.0 734.7 jit_solution(10359415230853190864)
XLA Ops:
  6.5 0.0 copy-start
  6.5 0.0 reduce-scatter.2.cloned.1.call-start
  6.5 0.8 compare_and_fusion
  7.4 1.7 gather_fusion
  9.1 0.0 copy-start.1
  9.1 0.7 copy-done.1
  9.8 0.1 broadcast_select_fusion.1
  9.9 16.8 %collective-permute-start = (bf16[3,2,2,64,128]{4,3,2,0,1:T(8,128)(2,1)S(1)}, bf16[3,2,2,64,128]{4,3,2,0,1:T(8,128)(2,1)S(1)}, u32[]{:S(2)}, u32[]{:S(2)}) collective-permute-start(bf16[3,2,2,64,128]{4,3,2,0,1:T(8,128)(2,1)S(1)} %broadcast_select_fusion.1), channel_id=1, source_target_pairs={{0,128},{128,256},{256,384},{1,129},{129,257},{257,385},{2,130},{1... | collective-permute-start | bytes 589832 | tf_op jit(solution)/shard_map/ppermute | solution.py:15
  26.7 0.0 copy-done
  26.7 1.9 gather_fusion.1
  28.6 0.6 collective-permute-done
  29.3 3.2 collective-permute-start.1
  32.5 1.3 collective-permute-start.2
  33.8 2.6 convolution_convert_fusion
  36.4 0.0 collective-permute-done.1
  36.4 2.5 collective-permute-done.2
  39.0 1.0 select_maximum_fusion
  40.0 0.0 copy-start.2
  40.0 0.1 pad_maximum_fusion
  40.1 0.2 fusion.34
  40.3 0.1 fusion.33
  40.3 0.2 fusion.32
  40.5 0.1 fusion.31
  40.6 0.2 fusion.29
  40.8 0.1 fusion.28
  40.8 0.2 fusion.26
  41.0 0.1 fusion.25
  41.1 0.2 fusion.22
  41.3 0.1 fusion.21
  41.3 0.2 fusion.19
  41.5 0.1 fusion.18
  41.6 0.2 fusion.16
  41.8 0.1 fusion.15
  41.8 0.0 copy-done.2
  41.8 0.1 fusion.37
  42.0 0.2 fusion.14
  42.1 0.1 fusion.13
  42.2 0.2 fusion.11
  42.4 2.9 convolution_bitcast_fusion
  45.3 4.0 copy.9
  49.4 4.7 reshape.13
  54.1 0.0 copy-start.3
  54.1 509.0 %all-reduce.2 = bf16[512,1728]{0,1:T(8,128)(2,1)} all-reduce(f32[512,1728]{0,1:T(8,128)} %reshape.13), channel_id=1, replica_groups=mesh['tm'=4,'height'=16,'panel'=8] {'tm','height'}, use_global_device_ids=true, to_apply=%region_0.1 | all-reduce | flops 884736 | bytes 5308416 | tf_op jit(solution)/shard_map/psum | solution.py:65
  563.1 3.2 fusion.38
  566.3 0.0 reduce-scatter.2.cloned.1.call-update
  566.3 160.1 %reduce-scatter.2.cloned.1.call-done = f32[64,216]{1,0:T(8,128)} async-done(((f32[512,216]{1,0:T(8,128)}), f32[64,216]{1,0:T(8,128)}) %reduce-scatter.2.cloned.1.call-update) | async-done | bytes 55312 | tf_op jit(solution)/shard_map/reduce_scatter | solution.py:68
  726.4 0.0 copy-done.3
  726.4 1.5 add_divide_fusion
  (11 shorter events, 0.3 us)
Async XLA Ops:
  6.5 20.2 %copy-start = (bf16[6,2,2,512,128]{4,3,2,1,0:T(8,128)(2,1)S(1)}, bf16[6,2,2,512,128]{4,3,2,1,0:T(8,128)(2,1)}, u32[]{:S(2)}) copy-start(bf16[6,2,2,512,128]{4,3,2,1,0:T(8,128)(2,1)} %param.7) | copy-start | bytes 9437188
  6.5 719.9 %reduce-scatter.2.cloned.1.call-start = ((), (), s32[]{:S(2)}) async-start(), calls=%async_computation.1 | async-start | bytes 589824 | tf_op jit(solution)/shard_map/reduce_scatter | solution.py:68
  9.1 0.7 copy-start.1
  9.9 19.4 %collective-permute-start = (bf16[3,2,2,64,128]{4,3,2,0,1:T(8,128)(2,1)S(1)}, bf16[3,2,2,64,128]{4,3,2,0,1:T(8,128)(2,1)S(1)}, u32[]{:S(2)}, u32[]{:S(2)}) collective-permute-start(bf16[3,2,2,64,128]{4,3,2,0,1:T(8,128)(2,1)S(1)} %broadcast_select_fusion.1), channel_id=1, source_target_pairs={{0,128},{128,256},{256,384},{1,129},{129,257},{257,385},{2,130},{1... | collective-permute-start | bytes 589832 | tf_op jit(solution)/shard_map/ppermute | solution.py:15
  29.3 7.1 collective-permute-start.1
  32.5 6.4 collective-permute-start.2
  40.0 1.9 copy-start.2
  54.1 672.3 %copy-start.3 = (f32[64,216]{1,0:T(8,128)S(1)}, f32[64,216]{1,0:T(8,128)}, u32[]{:S(2)}) copy-start(f32[64,216]{1,0:T(8,128)} %param.10) | copy-start | bytes 165892
Sparse Core Ops, SparseCore 0:
  566.4 159.9 reduce-scatter.1
where the time goes:
time: 740 us; the launch traced here: 735 us
  blocking collectives  509 us (69%)
  waiting for transfers between devices  163 us (22%)
  starting transfers between devices  21.3 us (3%)
  local copies, waits for them, and re-layouts  15.1 us (2%)
  between operations  13.7 us (2%)
  matrix products  8.69 us (1%)
    psum x1, blocking collectives, body(): summed = lax.psum(partial_grad, ('tm', 'height'))  509 us
    reduce_scatter x1, waiting for transfers between devices, body(): lax.psum_scatter(rotated, 'panel', scatter_dimension=0, tiled=True)  160 us
    ppermute x1, starting transfers between devices, from_behind(): lax.ppermute(value, axis, [(source, source + steps) for source in range(l...  16.8 us
  transfers between devices with their start and end apart: 4, of which 3 were waited for; matrix products, arithmetic and copies ran while one was open for 1% of the time, Pallas kernels for 0%

commit v1 on v0

--- a/solution.py
+++ b/solution.py
@@ -1,9 +1,20 @@
+import functools
+
 import jax
 import jax.numpy as jnp
+import numpy as np
 from jax import lax
+from jax.experimental import pallas as pl
+from jax.experimental.pallas import tpu as pltpu
 from jax.sharding import PartitionSpec as P
 
 FORGET = 3
+TAPS = 27
+LANES = 128
+SUB = 8
+CHIPS = 16
+PANELS = 8
+MESH = pl.DeviceIdType.MESH
 
 
 damping = 0.1
@@ -28,15 +39,266 @@
     return block
 
 
+def sum_kernel(
+    t_ref,
+    g_ref,
+    c_buf,
+    s_buf,
+    r_buf,
+    acc,
+    z_out,
+    z_in,
+    c_send,
+    c_recv,
+    s_send,
+    s_recv,
+    z_send,
+    z_recv,
+    g_send,
+    g_recv,
+    f_send,
+    f_recv,
+):
+    tm = lax.axis_index("tm")
+    me = lax.axis_index("height")
+    core = lax.rem(tm, 2)
+    mate = tm + 1 - 2 * core
+    far = lax.rem(tm + 2, 4)
+    rows = TAPS * SUB
+
+    barrier = pltpu.get_barrier_semaphore()
+    pl.semaphore_signal(barrier, inc=1, device_id={"tm": mate}, device_id_type=MESH)
+    pl.semaphore_signal(barrier, inc=1, device_id={"tm": far}, device_id_type=MESH)
+
+    @pl.loop(1, CHIPS)
+    def _(d):
+        pl.semaphore_signal(
+            barrier, inc=1, device_id={"height": lax.rem(me + d, CHIPS)}, device_id_type=MESH
+        )
+
+    pl.semaphore_wait(barrier, CHIPS + 1)
+
+    def c_rows(i):
+        return pl.ds(pl.multiple_of(lax.rem(me + i, SUB) * SUB, SUB), SUB)
+
+    def pair_copy(i):
+        half = pl.ds(pl.multiple_of((1 - core) * 256, 256), 256)
+        return pltpu.make_async_remote_copy(
+            src_ref=t_ref.at[:, c_rows(i), half],
+            dst_ref=c_buf.at[i],
+            send_sem=c_send.at[i],
+            recv_sem=c_recv.at[i],
+            device_id={"tm": mate},
+            device_id_type=MESH,
+        )
+
+    @pl.loop(0, SUB)
+    def _(i):
+        pair_copy(i).start()
+
+    def plane_copy(d):
+        return pltpu.make_async_remote_copy(
+            src_ref=s_buf.at[d],
+            dst_ref=r_buf.at[d],
+            send_sem=s_send.at[d],
+            recv_sem=s_recv.at[d],
+            device_id={"height": lax.rem(me + d, CHIPS)},
+            device_id_type=MESH,
+        )
+
+    def chunk(i, d):
+        low = lax.rem(me + d, CHIPS) // SUB
+        own = t_ref[
+            :, c_rows(i), pl.ds(pl.multiple_of((2 * core + low) * LANES, LANES), LANES)
+        ]
+        other = c_buf[i, :, :, pl.ds(pl.multiple_of(low * LANES, LANES), LANES)]
+        return (own + other).reshape(rows, LANES)
+
+    pair_copy(0).wait_recv()
+    s_buf[SUB] = chunk(0, SUB).astype(jnp.bfloat16)
+    plane_copy(SUB).start()
+    acc[...] = chunk(0, 0)
+
+    @pl.loop(1, SUB)
+    def _(i):
+        pair_copy(i).wait_recv()
+        s_buf[i] = chunk(i, i).astype(jnp.bfloat16)
+        plane_copy(i).start()
+        s_buf[i + SUB] = chunk(i, i + SUB).astype(jnp.bfloat16)
+        plane_copy(i + SUB).start()
+
+    @pl.loop(1, CHIPS)
+    def _(d):
+        plane_copy(d).wait_recv()
+        acc[...] += r_buf[d].astype(jnp.float32)
+
+    z_out[...] = acc[...].astype(jnp.bfloat16)
+    z_copy = pltpu.make_async_remote_copy(
+        src_ref=z_out,
+        dst_ref=z_in,
+        send_sem=z_send,
+        recv_sem=z_recv,
+        device_id={"tm": far},
+        device_id_type=MESH,
+    )
+    z_copy.start()
+    z_copy.wait_recv()
+
+    def slot(d):
+        owner = lax.rem(me - d + CHIPS, CHIPS)
+        return (2 * core + owner // SUB) * SUB + lax.rem(owner, SUB)
+
+    def gather_copy(d):
+        return pltpu.make_async_remote_copy(
+            src_ref=g_ref.at[slot(0)],
+            dst_ref=g_ref.at[slot(0)],
+            send_sem=g_send.at[d],
+            recv_sem=g_recv.at[d],
+            device_id={"height": lax.rem(me + d, CHIPS)},
+            device_id_type=MESH,
+        )
+
+    def hand_copy(d):
+        return pltpu.make_async_remote_copy(
+            src_ref=g_ref.at[slot(d)],
+            dst_ref=g_ref.at[slot(d)],
+            send_sem=f_send.at[d],
+            recv_sem=f_recv.at[d],
+            device_id={"tm": mate},
+            device_id_type=MESH,
+        )
+
+    g_ref[slot(0)] = (acc[...] + z_in[...].astype(jnp.float32)).astype(jnp.bfloat16)
+
+    @pl.loop(1, CHIPS)
+    def _(d):
+        gather_copy(d).start()
+
+    hand_copy(0).start()
+
+    @pl.loop(1, CHIPS)
+    def _(d):
+        gather_copy(d).wait_recv()
+        hand_copy(d).start()
+
+    @pl.loop(0, SUB)
+    def _(i):
+        pair_copy(i).wait_send()
+
+    z_copy.wait_send()
+    hand_copy(0).wait()
+
+    @pl.loop(1, CHIPS)
+    def _(d):
+        plane_copy(d).wait_send()
+        gather_copy(d).wait_send()
+        hand_copy(d).wait()
+
+
+def sum_gradient(partial):
+    rows = TAPS * SUB
+    dma = pltpu.SemaphoreType.DMA
+    return pl.pallas_call(
+        sum_kernel,
+        out_shape=jax.ShapeDtypeStruct((4 * SUB, rows, LANES), jnp.bfloat16),
+        in_specs=[pl.BlockSpec(memory_space=pltpu.VMEM)],
+        out_specs=pl.BlockSpec(memory_space=pltpu.VMEM),
+        scratch_shapes=[
+            pltpu.VMEM((SUB, TAPS, SUB, 2 * LANES), jnp.float32),
+            pltpu.VMEM((CHIPS, rows, LANES), jnp.bfloat16),
+            pltpu.VMEM((CHIPS, rows, LANES), jnp.bfloat16),
+            pltpu.VMEM((rows, LANES), jnp.float32),
+            pltpu.VMEM((rows, LANES), jnp.bfloat16),
+            pltpu.VMEM((rows, LANES), jnp.bfloat16),
+            dma((SUB,)),
+            dma((SUB,)),
+            dma((CHIPS,)),
+            dma((CHIPS,)),
+            dma(()),
+            dma(()),
+            dma((CHIPS,)),
+            dma((CHIPS,)),
+            dma((CHIPS,)),
+            dma((CHIPS,)),
+        ],
+        compiler_params=pltpu.CompilerParams(collective_id=0, has_side_effects=True),
+    )(partial)
+
+
+def panel_kernel(rot_ref, eig_ref, out_ref, s_buf, r_buf, s_send, s_recv):
+    me = lax.axis_index("panel")
+    barrier = pltpu.get_barrier_semaphore()
+
+    @pl.loop(1, PANELS)
+    def _(d):
+        pl.semaphore_signal(
+            barrier, inc=1, device_id={"panel": lax.rem(me + d, PANELS)}, device_id_type=MESH
+        )
+
+    pl.semaphore_wait(barrier, PANELS - 1)
+
+    def copy(d):
+        return pltpu.make_async_remote_copy(
+            src_ref=s_buf.at[d],
+            dst_ref=r_buf.at[d],
+            send_sem=s_send.at[d],
+            recv_sem=s_recv.at[d],
+            device_id={"panel": lax.rem(me + d, PANELS)},
+            device_id_type=MESH,
+        )
+
+    @pl.loop(1, PANELS)
+    def _(d):
+        s_buf[d] = rot_ref[lax.rem(me + d, PANELS)].astype(jnp.bfloat16)
+        copy(d).start()
+
+    out_ref[...] = rot_ref[me]
+
+    @pl.loop(1, PANELS)
+    def _(d):
+        copy(d).wait_recv()
+        out_ref[...] += r_buf[d].astype(jnp.float32)
+
+    out_ref[...] = out_ref[...] / (eig_ref[...] + damping)
+
+    @pl.loop(1, PANELS)
+    def _(d):
+        copy(d).wait_send()
+
+
+def finish(rotated, eigenvalues):
+    _, height, width = rotated.shape
+    vmem = pl.BlockSpec(memory_space=pltpu.VMEM)
+    return pl.pallas_call(
+        panel_kernel,
+        out_shape=jax.ShapeDtypeStruct((height, width), jnp.float32),
+        in_specs=[vmem, vmem],
+        out_specs=vmem,
+        scratch_shapes=[
+            pltpu.VMEM((PANELS, height, width), jnp.bfloat16),
+            pltpu.VMEM((PANELS, height, width), jnp.bfloat16),
+            pltpu.SemaphoreType.DMA((PANELS,)),
+            pltpu.SemaphoreType.DMA((PANELS,)),
+        ],
+        compiler_params=pltpu.CompilerParams(collective_id=1, has_side_effects=True),
+    )(rotated, eigenvalues)
+
+
+def tap_major(in_basis):
+    block = TAPS * SUB
+    source = np.arange(block).reshape(SUB, TAPS).T.reshape(-1)
+    pick = jnp.asarray(np.eye(block, dtype=np.float32)[source], jnp.bfloat16)
+    blocks = in_basis.reshape(-1, block, in_basis.shape[1])
+    return jnp.einsum("sr,brj->bsj", pick, blocks, preferred_element_type=jnp.bfloat16)
+
+
 def body(activations, out_grad, out_basis, in_basis, eigenvalues, forget_order):
     chosen = forget_order[:FORGET]
     sel_act = jnp.take(activations, chosen, axis=0)
     sel_grad = jnp.take(out_grad, chosen, axis=0)
     frames = sel_act.shape[1]
     rows = sel_act.shape[2]
-    channels = sel_act.shape[3]
     wide = sel_act.shape[4]
-    outputs = sel_grad.shape[3]
     projected = jnp.einsum(
         "nfrow,ok->nfrkw", sel_grad, out_basis, preferred_element_type=jnp.float32
     ).astype(jnp.bfloat16)
@@ -59,14 +321,15 @@
                 )
     stacked = jnp.stack(windows, axis=0)
     partial_grad = jnp.einsum(
-        "nfrkw,tnfrcw->kct", projected, stacked, preferred_element_type=jnp.float32
+        "nfrkw,tnfrcw->tck", projected, stacked, preferred_element_type=jnp.float32
     )
-    partial_grad = partial_grad.reshape(outputs, channels * 27)
-    summed = lax.psum(partial_grad, ("tm", "height"))
-    grad = summed.astype(jnp.bfloat16)
-    rotated = jnp.dot(grad, in_basis, preferred_element_type=jnp.float32)
-    reduced = lax.psum_scatter(rotated, "panel", scatter_dimension=0, tiled=True)
-    return reduced / (eigenvalues + damping)
+    grad = sum_gradient(partial_grad)
+    basis = tap_major(in_basis)
+    grad = grad.reshape(4, in_basis.shape[0], LANES)
+    basis = basis.reshape(in_basis.shape)
+    rotated = jnp.einsum("ark,rj->akj", grad, basis, preferred_element_type=jnp.float32)
+    rotated = rotated.reshape(PANELS, -1, in_basis.shape[1])
+    return finish(rotated, eigenvalues)
 
 
 def solution(mesh):

time: 740 us -> 127 us (0.17)
  the two profiles are of different devices: /device:TPU:1 before, /device:TPU:56 now
where the time goes in v1:
time: 127 us
  Pallas kernels  85.7 us (67%)
  local copies, waits for them, and re-layouts  13.8 us (11%)
  matrix products  11.9 us (9%)
  starting transfers between devices  7.59 us (6%)
  waiting for transfers between devices  5.5 us (4%)
  other arithmetic  2.14 us (2%)
    pallas_call x1, Pallas kernels, sum_gradient(): pl.pallas_call(sum_kernel, out_shape=jax.ShapeDtypeStruct((4 * SUB, rows,...  67.1 us
    pallas_call x1, Pallas kernels, finish(): pl.pallas_call(panel_kernel, out_shape=jax.ShapeDtypeStruct((height, widt...  18.6 us
    ppermute x1, waiting for transfers between devices, with_halo(): lax.ppermute(lax.slice_in_dim(block, 0, width, axis=dim), axis, backward)  5.18 us
    dot_general x1, matrix products, body(): jnp.einsum('nfrkw,tnfrcw->tck', projected, stacked, preferred_element_typ...  4.74 us
    unnamed x35, local copies, waits for them, and re-layouts  4.01 us
    dot_general x1, local copies, waits for them, and re-layouts, body(): jnp.einsum('ark,rj->akj', grad, basis, preferred_element_type=jnp.float32)  3.81 us
    dot_general x1, matrix products, body(): jnp.einsum('ark,rj->akj', grad, basis, preferred_element_type=jnp.float32)  3.15 us
    ppermute x1, starting transfers between devices, with_halo(): lax.ppermute(lax.slice_in_dim(block, block.shape[dim] - width, None, axis...  3.06 us
  transfers between devices with their start and end apart: 3, of which 2 were waited for; matrix products, arithmetic and copies ran while one was open for 6% of the time, Pallas kernels for 0%

profile of v1, /device:TPU:56, one launch (start us, length us, event | category | flops | bytes accessed | tf_op | source)
XLA Modules:
  0.0 127.0 jit_solution(654624382413976078)
XLA Ops:
  0.0 0.0 copy-start
  0.0 0.8 compare_and_fusion
  0.8 1.7 %gather_fusion = bf16[3,2,2,64,128]{4,3,2,1,0:T(8,128)(2,1)S(1)} fusion(bf16[6,2,2,64,128]{4,3,2,1,0:T(8,128)(2,1)} %param.7, s32[1024]{0:T(1024)S(1)} %pad_clamp_fusion), kind=kCustom, calls=%fused_computation | custom fusion | bytes 393228 | tf_op jit(solution)/shard_map/jit(_take)/gather | solution.py:297
  2.5 0.0 copy-start.2
  2.6 0.7 copy-done.2
  3.2 0.1 broadcast_select_fusion.1
  3.3 1.8 %collective-permute-start = (bf16[3,2,2,64,128]{4,3,2,0,1:T(8,128)(2,1)S(1)}, bf16[3,2,2,64,128]{4,3,2,0,1:T(8,128)(2,1)S(1)}, u32[]{:S(2)}, u32[]{:S(2)}) collective-permute-start(bf16[3,2,2,64,128]{4,3,2,0,1:T(8,128)(2,1)S(1)} %broadcast_select_fusion.1), channel_id=1, source_target_pairs={{0,128},{128,256},{256,384},{1,129},{129,257},{257,385},{2,130},{1... | collective-permute-start | bytes 589832 | tf_op jit(solution)/shard_map/ppermute | solution.py:26
  5.1 0.0 copy-done
  5.1 2.0 %gather_fusion.1 = bf16[3,2,2,512,128]{4,3,2,1,0:T(8,128)(2,1)} fusion(bf16[6,2,2,512,128]{4,3,2,1,0:T(8,128)(2,1)S(1)} %copy-done, s32[1024]{0:T(1024)S(1)} %pad_clamp_fusion), kind=kCustom, calls=%fused_computation.1 | custom fusion | bytes 3145740 | tf_op jit(solution)/shard_map/jit(_take)/gather | solution.py:298
  7.0 2.2 %copy.22 = bf16[1728,216]{1,0:T(8,128)(2,1)} copy(bf16[1728,216]{0,1:T(8,128)(2,1)} %param.10) | data formatting | bytes 1492992 | tf_op jit(solution)/shard_map/reshape | solution.py:291
  9.2 0.0 copy-start.1
  9.2 0.0 copy-start.4
  9.2 2.7 %convolution_convert_fusion = bf16[3,2,2,128,512]{3,4,2,0,1:T(8,128)(2,1)S(1)} fusion(bf16[512,512]{1,0:T(8,128)(2,1)} %param.9, bf16[3,2,2,512,128]{4,3,2,1,0:T(8,128)(2,1)} %gather_fusion.1, pred[3]{0:T(512)(128)(4,1)S(1)} %get-tuple-element.5), kind=kOutput, calls=%fused_computation.6 | convolution fusion | flops 806879232 | bytes 3670019 | tf_op jit(solution)/shard_map/nfrow,ok->nfrkw/dot_general | solution.py:302
  11.9 0.0 collective-permute-done
  11.9 3.1 %collective-permute-start.1 = (bf16[3,4,1,64,128]{4,3,2,0,1:T(8,128)(2,1)S(1)}, bf16[3,4,1,64,128]{4,3,2,0,1:T(8,128)(2,1)S(1)}, u32[]{:S(2)}, u32[]{:S(2)}) collective-permute-start(bf16[3,4,1,64,128]{4,3,2,0,1:T(8,128)(2,1)S(1)} %get-tuple-element.9), channel_id=1, source_target_pairs={{0,8},{8,16},{16,24},{24,32},{32,40},{40,48},{48,56},{56,64},{64,7... | collective-permute-start | bytes 589832 | tf_op jit(solution)/shard_map/ppermute | solution.py:34
  15.0 2.8 %collective-permute-start.2 = (bf16[3,4,1,64,128]{4,3,2,0,1:T(8,128)(2,1)S(1)}, bf16[3,4,1,64,128]{4,3,2,0,1:T(8,128)(2,1)S(1)}, u32[]{:S(2)}, u32[]{:S(2)}) collective-permute-start(bf16[3,4,1,64,128]{4,3,2,0,1:T(8,128)(2,1)S(1)} %get-tuple-element.10), channel_id=1, source_target_pairs={{8,0},{16,8},{24,16},{32,24},{40,32},{48,40},{56,48},{64,56},{72,6... | collective-permute-start | bytes 589832 | tf_op jit(solution)/shard_map/ppermute | solution.py:37
  17.8 0.0 copy-done.1
  17.8 0.0 copy-done.4
  17.8 1.4 %fusion.36 = bf16[216,8,216]{2,0,1:T(8,128)(2,1)} fusion(bf16[216,216,1]{1,0,2:T(8,128)(2,1)S(1)} %copy-done.4, bf16[8,216,216]{2,1,0:T(8,128)(2,1)S(1)} %bitcast.143), kind=kOutput, calls=%fused_computation.82 | convolution fusion | flops 161243136 | bytes 1586304 | tf_op jit(solution)/shard_map/sr,brj->bsj/dot_general | solution.py:292
  19.2 0.3 collective-permute-done.1
  19.5 5.2 %collective-permute-done.2 = bf16[3,4,1,64,128]{4,3,2,0,1:T(8,128)(2,1)S(1)} collective-permute-done((bf16[3,4,1,64,128]{4,3,2,0,1:T(8,128)(2,1)S(1)}, bf16[3,4,1,64,128]{4,3,2,0,1:T(8,128)(2,1)S(1)}, u32[]{:S(2)}, u32[]{:S(2)}) %collective-permute-start.2) | collective-permute-done | bytes 196640 | tf_op jit(solution)/shard_map/ppermute | solution.py:37
  24.7 1.0 select_maximum_fusion
  25.7 0.0 copy-start.3
  25.7 0.1 pad_maximum_fusion
  25.8 0.2 fusion.32
  26.0 0.1 fusion.31
  26.1 0.2 fusion.30
  26.2 0.1 fusion.29
  26.3 0.2 fusion.27
  26.5 0.1 fusion.26
  26.6 0.2 fusion.24
  26.7 0.1 fusion.23
  26.8 0.2 fusion.20
  27.0 0.1 fusion.19
  27.1 0.2 fusion.17
  27.2 0.1 fusion.16
  27.3 0.2 fusion.14
  27.5 0.1 fusion.13
  27.6 0.0 copy-done.3
  27.6 0.1 fusion.35
  27.7 0.2 fusion.12
  27.9 0.1 fusion.11
  28.0 0.2 fusion.9
  28.1 4.7 %convolution_bitcast_fusion.t_ref = f32[27,64,512]{2,1,0:T(8,128)} fusion(bf16[27,3,2,2,64,128]{5,4,3,1,2,0:T(8,128)(2,1)S(1)} %fusion.9, bf16[3,2,2,128,512]{3,4,2,0,1:T(8,128)(2,1)S(1)} %convolution_convert_fusion), kind=kOutput, calls=%fused_computation.5 | convolution fusion | flops 2717908992 | bytes 10420224 | tf_op jit(solution)/shard_map/nfrkw,tnfrcw->tck/dot_general | solution.py:323
  32.9 67.1 %shard_map.73 = bf16[32,216,128]{2,1,0:T(8,128)(2,1)} custom-call(f32[27,64,512]{2,1,0:T(8,128)} %convolution_bitcast_fusion.t_ref), custom_call_target="tpu_custom_call" | custom-call | tf_op jit(solution)/shard_map/pallas_call | solution.py:201
  100.0 3.8 %copy.13 = bf16[4,128,1728]{2,1,0:T(8,128)(2,1)} copy(bf16[4,128,1728]{1,2,0:T(8,128)(2,1)} %bitcast.142) | data formatting | bytes 3538944 | tf_op jit(solution)/shard_map/ark,rj->akj/dot_general | solution.py:330
  103.8 3.2 %fusion.37.rot_ref = f32[8,64,216]{2,1,0:T(8,128)} fusion(bf16[8,64,1728]{2,1,0:T(8,128)(2,1)} %bitcast.144, bf16[1728,216,1]{1,0,2:T(8,128)(2,1)} %bitcast.145), kind=kOutput, calls=%fused_computation.83 | convolution fusion | flops 382205952 | bytes 2958336 | tf_op jit(solution)/shard_map/ark,rj->akj/dot_general | solution.py:330
  107.0 18.6 %shard_map.74 = f32[64,216]{1,0:T(8,128)} custom-call(f32[8,64,216]{2,1,0:T(8,128)} %fusion.37.rot_ref, f32[64,216]{1,0:T(8,128)} %eig_ref.1), custom_call_target="tpu_custom_call" | custom-call | tf_op jit(solution)/shard_map/pallas_call | solution.py:272
  125.6 1.5 %copy.55 = f32[64,216]{1,0:T(8,128)} copy(f32[64,216]{1,0:T(8,128)} %shard_map.74) | data formatting | bytes 110592
  (11 shorter events, 0.3 us)
Async XLA Ops:
  0.0 5.1 %copy-start = (bf16[6,2,2,512,128]{4,3,2,1,0:T(8,128)(2,1)S(1)}, bf16[6,2,2,512,128]{4,3,2,1,0:T(8,128)(2,1)}, u32[]{:S(2)}) copy-start(bf16[6,2,2,512,128]{4,3,2,1,0:T(8,128)(2,1)} %param.8) | copy-start | bytes 9437188
  2.5 0.7 copy-start.2
  3.3 8.6 %collective-permute-start = (bf16[3,2,2,64,128]{4,3,2,0,1:T(8,128)(2,1)S(1)}, bf16[3,2,2,64,128]{4,3,2,0,1:T(8,128)(2,1)S(1)}, u32[]{:S(2)}, u32[]{:S(2)}) collective-permute-start(bf16[3,2,2,64,128]{4,3,2,0,1:T(8,128)(2,1)S(1)} %broadcast_select_fusion.1), channel_id=1, source_target_pairs={{0,128},{128,256},{256,384},{1,129},{129,257},{257,385},{2,130},{1... | collective-permute-start | bytes 589832 | tf_op jit(solution)/shard_map/ppermute | solution.py:26
  9.2 8.6 %copy-start.1 = (bf16[1728,216]{1,0:T(8,128)(2,1)S(1)}, bf16[1728,216]{1,0:T(8,128)(2,1)}, u32[]{:S(2)}) copy-start(bf16[1728,216]{1,0:T(8,128)(2,1)} %copy.22) | copy-start | bytes 2239492
  9.2 8.6 %copy-start.4 = (bf16[216,216,1]{1,0,2:T(8,128)(2,1)S(1)}, bf16[216,216,1]{1,0,2:T(8,128)(2,1)}, u32[]{:S(2)}) copy-start(bf16[216,216,1]{1,0,2:T(8,128)(2,1)} %constant.40) | copy-start | bytes 279940
  11.9 7.6 %collective-permute-start.1 = (bf16[3,4,1,64,128]{4,3,2,0,1:T(8,128)(2,1)S(1)}, bf16[3,4,1,64,128]{4,3,2,0,1:T(8,128)(2,1)S(1)}, u32[]{:S(2)}, u32[]{:S(2)}) collective-permute-start(bf16[3,4,1,64,128]{4,3,2,0,1:T(8,128)(2,1)S(1)} %get-tuple-element.9), channel_id=1, source_target_pairs={{0,8},{8,16},{16,24},{24,32},{32,40},{40,48},{48,56},{56,64},{64,7... | collective-permute-start | bytes 589832 | tf_op jit(solution)/shard_map/ppermute | solution.py:34
  15.0 9.7 %collective-permute-start.2 = (bf16[3,4,1,64,128]{4,3,2,0,1:T(8,128)(2,1)S(1)}, bf16[3,4,1,64,128]{4,3,2,0,1:T(8,128)(2,1)S(1)}, u32[]{:S(2)}, u32[]{:S(2)}) collective-permute-start(bf16[3,4,1,64,128]{4,3,2,0,1:T(8,128)(2,1)S(1)} %get-tuple-element.10), channel_id=1, source_target_pairs={{8,0},{16,8},{24,16},{32,24},{40,32},{48,40},{56,48},{64,56},{72,6... | collective-permute-start | bytes 589832 | tf_op jit(solution)/shard_map/ppermute | solution.py:37
  25.7 1.9 %copy-start.3 = (bf16[3,2,2,64,128]{4,3,2,1,0:T(8,128)(2,1)S(1)}, bf16[3,2,2,64,128]{4,3,2,1,0:T(8,128)(2,1)}, u32[]{:S(2)}) copy-start(bf16[3,2,2,64,128]{4,3,2,1,0:T(8,128)(2,1)} %copy-done.2) | copy-start | bytes 589828

commit v2 on v0

v2 whole, which is shorter than its diff:
```python
import jax
import jax.numpy as jnp
from jax import lax
from jax.experimental import pallas as pl
from jax.experimental.pallas import tpu as pltpu
from jax.sharding import PartitionSpec as P

FORGET = 3
TAPS = 27
LANES = 128
SUB = 8
SLABS = 4
CHIPS = 16
PANELS = 8
BLOCKS = 12
CHANNELS = 64
OUT = 512
ROWS = TAPS * SUB
MESH = pl.DeviceIdType.MESH


damping = 0.1


def kernel(
    order_ref,
    act_ref,
    grad_ref,
    ob_ref,
    bt_ref,
    eig_ref,
    out_ref,
    e_buf,
    w_buf,
    p_buf,
    t_buf,
    c_buf,
    s_buf,
    r_buf,
    acc,
    z_out,
    z_in,
    g_buf,
    b_buf,
    rot_buf,
    fin_buf,
    q_buf,
    y_buf,
    h_send,
    h_recv,
    c_send,
    c_recv,
    s_send,
    s_recv,
    z_send,
    z_recv,
    g_send,
    g_recv,
    f_send,
    f_recv,
    q_send,
    q_recv,
):
    tm = lax.axis_index("tm")
    me = lax.axis_index("height")
    panel = lax.axis_index("panel")
    core = lax.rem(tm, 2)
    mate = tm + 1 - 2 * core
    far = lax.rem(tm + 2, SLABS)
    up = lax.rem(me + 1, CHIPS)
    down = lax.rem(me + CHIPS - 1, CHIPS)

    barrier = pltpu.get_barrier_semaphore()
    for axis, mine, count in (("tm", tm, SLABS), ("height", me, CHIPS), ("panel", panel, PANELS)):

        @pl.loop(1, count)
        def _(d):
            pl.semaphore_signal(
                barrier, inc=1, device_id={axis: lax.rem(mine + d, count)}, device_id_type=MESH
            )

    for n in range(FORGET):
        e_buf[n, 2:4, 1:3] = act_ref[order_ref[n]]

    @pl.when(tm == 0)
    def _():
        e_buf[:, 0:2] = jnp.zeros_like(e_buf[:, 0:2])

    @pl.when(me == 0)
    def _():
        e_buf[:, :, 0:1] = jnp.zeros_like(e_buf[:, :, 0:1])

    @pl.when(me == CHIPS - 1)
    def _():
        e_buf[:, :, 3:4] = jnp.zeros_like(e_buf[:, :, 3:4])

    def halo(i):
        source, target, device = (
            ((slice(2, 4), slice(1, 3)), (slice(0, 2), slice(1, 3)), {"tm": lax.rem(tm + 1, SLABS)}),
            ((slice(2, 4), slice(2, 3)), (slice(2, 4), slice(0, 1)), {"height": up}),
            ((slice(2, 4), slice(1, 2)), (slice(2, 4), slice(3, 4)), {"height": down}),
            ((slice(0, 2), slice(2, 3)), (slice(0, 2), slice(0, 1)), {"height": up}),
            ((slice(0, 2), slice(1, 2)), (slice(0, 2), slice(3, 4)), {"height": down}),
        )[i]
        return pltpu.make_async_remote_copy(
            src_ref=e_buf.at[(slice(None),) + source],
            dst_ref=e_buf.at[(slice(None),) + target],
            send_sem=h_send.at[i],
            recv_sem=h_recv.at[i],
            device_id=device,
            device_id_type=MESH,
        )

    sends = (
        tm < SLABS - 1,
        me < CHIPS - 1,
        me > 0,
        jnp.logical_and(tm > 0, me < CHIPS - 1),
        jnp.logical_and(tm > 0, me > 0),
    )
    receives = (
        tm > 0,
        me > 0,
        me < CHIPS - 1,
        jnp.logical_and(tm > 0, me > 0),
        jnp.logical_and(tm > 0, me < CHIPS - 1),
    )

    pl.semaphore_wait(barrier, SLABS + CHIPS + PANELS - 3)
    for i in range(3):

        @pl.when(sends[i])
        def _():
            halo(i).start()

    @pl.loop(0, BLOCKS)
    def _(b):
        block = grad_ref[order_ref[b // 4], lax.rem(b // 2, 2), lax.rem(b, 2)]
        rows = pl.ds(pl.multiple_of(b * LANES, LANES), LANES)
        p_buf[rows, :] = lax.dot_general(
            block, ob_ref[...], (((0,), (0,)), ((), ())), preferred_element_type=jnp.float32
        ).astype(jnp.bfloat16)

    def half(which):
        return pl.ds(pl.multiple_of(which * 2 * LANES, 2 * LANES), 2 * LANES)

    def pair_copy(dt):
        return pltpu.make_async_remote_copy(
            src_ref=t_buf.at[pl.ds(dt * 9, 9), :, half(1 - core)],
            dst_ref=c_buf.at[pl.ds(dt * 9, 9)],
            send_sem=c_send.at[dt],
            recv_sem=c_recv.at[dt],
            device_id={"tm": mate},
            device_id_type=MESH,
        )

    column = lax.broadcasted_iota(jnp.int32, (CHANNELS, LANES), 1)

    def taps_of(dt):
        @pl.loop(0, BLOCKS)
        def _(b):
            n, f, r = b // 4, lax.rem(b // 2, 2), lax.rem(b, 2)
            lanes = pl.ds(pl.multiple_of(b * LANES, LANES), LANES)
            for dh in range(3):
                tile = e_buf[n, f + dt, r + dh]
                wide = tile.astype(jnp.float32)
                left = jnp.where(column == 0, 0.0, pltpu.roll(wide, 1, 1)).astype(jnp.bfloat16)
                right = jnp.where(column == LANES - 1, 0.0, pltpu.roll(wide, LANES - 1, 1)).astype(
                    jnp.bfloat16
                )
                for dw, shifted in enumerate((left, tile, right)):
                    at = (dt * 9 + dh * 3 + dw) * CHANNELS
                    w_buf[at : at + CHANNELS, lanes] = shifted

        at = dt * 9 * CHANNELS
        t_buf[dt * 9 : dt * 9 + 9] = jnp.dot(
            w_buf[at : at + 9 * CHANNELS, :], p_buf[...], preferred_element_type=jnp.float32
        ).reshape(9, CHANNELS, OUT)
        pair_copy(dt).start()

    for i in (1, 2):

        @pl.when(receives[i])
        def _():
            halo(i).wait_recv()

    taps_of(2)

    for cb in range(SUB):
        first = cb * ROWS // LANES * LANES
        last = min(first + 3 * LANES, bt_ref.shape[1])
        row = lax.broadcasted_iota(jnp.int32, (last - first, ROWS), 0)
        col = lax.broadcasted_iota(jnp.int32, (last - first, ROWS), 1)
        wanted = cb * ROWS - first + lax.rem(col, SUB) * TAPS + col // SUB
        pick = jnp.where(row == wanted, 1.0, 0.0).astype(jnp.bfloat16)
        b_buf[cb] = jnp.dot(
            bt_ref[:, first:last], pick, preferred_element_type=jnp.float32
        ).astype(jnp.bfloat16)
    rot_buf[...] = jnp.zeros_like(rot_buf)

    @pl.when(receives[0])
    def _():
        halo(0).wait_recv()

    for i in (3, 4):

        @pl.when(sends[i])
        def _():
            halo(i).start()

    for i in (3, 4):

        @pl.when(receives[i])
        def _():
            halo(i).wait_recv()

    taps_of(1)
    taps_of(0)

    def plane_copy(d):
        return pltpu.make_async_remote_copy(
            src_ref=s_buf.at[d],
            dst_ref=r_buf.at[d],
            send_sem=s_send.at[d],
            recv_sem=s_recv.at[d],
            device_id={"height": lax.rem(me + d, CHIPS)},
            device_id_type=MESH,
        )

    def chunk(d):
        chip = lax.rem(me + d, CHIPS)
        low = chip // SUB
        rows = pl.ds(pl.multiple_of(lax.rem(chip, SUB) * SUB, SUB), SUB)
        own = t_buf[:, rows, pl.ds(pl.multiple_of((2 * core + low) * LANES, LANES), LANES)]
        other = c_buf[:, rows, pl.ds(pl.multiple_of(low * LANES, LANES), LANES)]
        return (own + other).reshape(ROWS, LANES)

    for dt in (2, 1, 0):
        pair_copy(dt).wait_recv()

    @pl.loop(1, CHIPS)
    def _(d):
        s_buf[d] = chunk(d).astype(jnp.bfloat16)
        plane_copy(d).start()

    acc[...] = chunk(0)

    @pl.loop(1, CHIPS)
    def _(d):
        plane_copy(d).wait_recv()
        acc[...] += r_buf[d].astype(jnp.float32)

    z_out[...] = acc[...].astype(jnp.bfloat16)
    z_copy = pltpu.make_async_remote_copy(
        src_ref=z_out,
        dst_ref=z_in,
        send_sem=z_send,
        recv_sem=z_recv,
        device_id={"tm": far},
        device_id_type=MESH,
    )
    z_copy.start()
    z_copy.wait_recv()

    def place(which, d):
        owner = lax.rem(me - d + CHIPS, CHIPS)
        return 2 * which + owner // SUB, lax.rem(owner, SUB)

    def gather_copy(d):
        kb, cb = place(core, 0)
        return pltpu.make_async_remote_copy(
            src_ref=g_buf.at[kb, cb],
            dst_ref=g_buf.at[kb, cb],
            send_sem=g_send.at[d],
            recv_sem=g_recv.at[d],
            device_id={"height": lax.rem(me + d, CHIPS)},
            device_id_type=MESH,
        )

    def hand_copy(d):
        kb, cb = place(core, d)
        return pltpu.make_async_remote_copy(
            src_ref=g_buf.at[kb, cb],
            dst_ref=g_buf.at[kb, cb],
            send_sem=f_send.at[d],
            recv_sem=f_recv.at[d],
            device_id={"tm": mate},
            device_id_type=MESH,
        )

    def rotate(which, d):
        kb, cb = place(which, d)
        rot_buf[kb] += jnp.dot(b_buf[cb], g_buf[kb, cb], preferred_element_type=jnp.float32)

    kb0, cb0 = place(core, 0)
    g_buf[kb0, cb0] = (acc[...] + z_in[...].astype(jnp.float32)).astype(jnp.bfloat16)

    @pl.loop(1, CHIPS)
    def _(d):
        gather_copy(d).start()

    hand_copy(0).start()
    rotate(core, 0)

    @pl.loop(1, CHIPS)
    def _(d):
        gather_copy(d).wait_recv()
        hand_copy(d).start()
        rotate(core, d)

    @pl.loop(0, CHIPS)
    def _(d):
        hand_copy(d).wait_recv()
        rotate(1 - core, d)

    for kb in range(4):
        fin_buf[2 * kb : 2 * kb + 2] = rot_buf[kb].T.reshape(2, CHANNELS, ROWS)

    def panel_copy(d):
        return pltpu.make_async_remote_copy(
            src_ref=q_buf.at[d],
            dst_ref=y_buf.at[d],
            send_sem=q_send.at[d],
            recv_sem=q_recv.at[d],
            device_id={"panel": lax.rem(panel + d, PANELS)},
            device_id_type=MESH,
        )

    @pl.loop(1, PANELS)
    def _(d):
        q_buf[d] = fin_buf[lax.rem(panel + d, PANELS)].astype(jnp.bfloat16)
        panel_copy(d).start()

    out_ref[...] = fin_buf[panel]

    @pl.loop(1, PANELS)
    def _(d):
        panel_copy(d).wait_recv()
        out_ref[...] += y_buf[d].astype(jnp.float32)

    out_ref[...] = out_ref[...] / (eig_ref[...] + damping)

    for i in range(5):

        @pl.when(sends[i])
        def _():
            halo(i).wait_send()

    for dt in range(3):
        pair_copy(dt).wait_send()
    z_copy.wait_send()
    hand_copy(0).wait_send()

    @pl.loop(1, CHIPS)
    def _(d):
        plane_copy(d).wait_send()
        gather_copy(d).wait_send()
        hand_copy(d).wait_send()

    @pl.loop(1, PANELS)
    def _(d):
        panel_copy(d).wait_send()


def body(activations, out_grad, out_basis, in_basis, eigenvalues, forget_order):
    dma = pltpu.SemaphoreType.DMA
    bf16, f32 = jnp.bfloat16, jnp.float32
    vmem = pl.BlockSpec(memory_space=pltpu.VMEM)
    positions = BLOCKS * LANES
    return pl.pallas_call(
        kernel,
        out_shape=jax.ShapeDtypeStruct(eigenvalues.shape, f32),
        in_specs=[pl.BlockSpec(memory_space=pltpu.SMEM)] + [vmem] * 5,
        out_specs=vmem,
        scratch_shapes=[
            pltpu.VMEM((FORGET, 4, 4, CHANNELS, LANES), bf16),
            pltpu.VMEM((TAPS * CHANNELS, positions), bf16),
            pltpu.VMEM((positions, OUT), bf16),
            pltpu.VMEM((TAPS, CHANNELS, OUT), f32),
            pltpu.VMEM((TAPS, CHANNELS, OUT // 2), f32),
            pltpu.VMEM((CHIPS, ROWS, LANES), bf16),
            pltpu.VMEM((CHIPS, ROWS, LANES), bf16),
            pltpu.VMEM((ROWS, LANES), f32),
            pltpu.VMEM((ROWS, LANES), bf16),
            pltpu.VMEM((ROWS, LANES), bf16),
            pltpu.VMEM((4, SUB, ROWS, LANES), bf16),
            pltpu.VMEM((SUB, ROWS, ROWS), bf16),
            pltpu.VMEM((4, ROWS, LANES), f32),
            pltpu.VMEM((PANELS, CHANNELS, ROWS), f32),
            pltpu.VMEM((PANELS, CHANNELS, ROWS), bf16),
            pltpu.VMEM((PANELS, CHANNELS, ROWS), bf16),
            dma((5,)),
            dma((5,)),
            dma((3,)),
            dma((3,)),
            dma((CHIPS,)),
            dma((CHIPS,)),
            dma(()),
            dma(()),
            dma((CHIPS,)),
            dma((CHIPS,)),
            dma((CHIPS,)),
            dma((CHIPS,)),
            dma((PANELS,)),
            dma((PANELS,)),
        ],
        compiler_params=pltpu.CompilerParams(
            collective_id=0, has_side_effects=True, vmem_limit_bytes=56 * 1024 * 1024
        ),
    )(forget_order, activations, out_grad, out_basis, in_basis.T, eigenvalues)


def solution(mesh):
    in_specs = (
        P(None, "tm", "height", "panel", None),
        P(None, "tm", "height", None, None),
        P(),
        P("panel", ("tm", "height")),
        P("panel", ("tm", "height")),
        P(),
    )
    out_specs = P("panel", ("tm", "height"))
    return jax.shard_map(body, mesh=mesh, in_specs=in_specs, out_specs=out_specs, check_vma=False)
```

time: 740 us -> 92.5 us (0.12)
  blocking collectives: 509 us -> 0 us
  waiting for transfers between devices: 163 us -> 0 us
  Pallas kernels: 0 us -> 89.2 us
  starting transfers between devices: 21.3 us -> 0 us
  between operations: 13.7 us -> 0.01 us
  local copies, waits for them, and re-layouts: 15.1 us -> 1.47 us
  matrix products: 8.69 us -> 0 us
    psum x1 -> x0, blocking collectives: 509 us -> none  [body(): summed = lax.psum(partial_grad, ('tm', 'height'))]
    reduce_scatter x1 -> x0, waiting for transfers between devices: 160 us -> none  [body(): lax.psum_scatter(rotated, 'panel', scatter_dimension=0, tiled=True)]
    pallas_call x0 -> x1, Pallas kernels: none -> 89.2 us  [body(): pl.pallas_call(kernel, out_shape=jax.ShapeDtypeStruct(eigenvalues.shape,...]
    ppermute x3 -> x0, starting transfers between devices: 21.3 us -> none  [the longest x1 16.8 us: from_behind(): lax.ppermute(value, axis, [(source, source + steps) for source in range(l...]
    dot_general x3 -> x0, matrix products: 8.69 us -> none  [the longest x1 3.17 us: body(): rotated = jnp.dot(grad, in_basis, preferred_element_type=jnp.float32)]
  transfers between devices with their start and end apart: 4 -> 0, of which waited for: 3 -> 0; matrix products, arithmetic and copies ran while one was open for 1% -> 0% of each run, Pallas kernels for 0% -> 0%
where the time goes in v2:
time: 92.5 us; the launch traced here: 90.7 us
  Pallas kernels  89.2 us (96%)
  local copies, waits for them, and re-layouts  1.47 us (2%)
    pallas_call x1, Pallas kernels, body(): pl.pallas_call(kernel, out_shape=jax.ShapeDtypeStruct(eigenvalues.shape,...  89.2 us

profile of v2, /device:TPU:1, one launch (start us, length us, event | category | flops | bytes accessed | tf_op | source)
XLA Modules:
  0.0 90.7 jit_solution(960786826225164537)
XLA Ops:
  0.0 89.2 %shard_map.64 = f32[64,216]{1,0:T(8,128)} custom-call(s32[6]{0:T(128)} %order_ref.1, bf16[6,2,2,64,128]{4,3,2,1,0:T(8,128)(2,1)} %act_ref.1, bf16[6,2,2,512,128]{4,3,2,1,0:T(8,128)(2,1)} %grad_ref.1, bf16[512,512]{1,0:T(8,128)(2,1)} %ob_ref.1, bf16[216,1728]{1,0:T(8,128)(2,1)} %bitcast.1, f32[64,216]{1,0:T(8,128)} %eig_ref.1), custom_call_target="tpu_custom_call" | custom-call | tf_op jit(solution)/shard_map/pallas_call | solution.py:370
  89.2 1.5 %copy.8 = f32[64,216]{1,0:T(8,128)} copy(f32[64,216]{1,0:T(8,128)} %shard_map.64) | data formatting | bytes 110592

commit v3 on v2

--- a/solution.py
+++ b/solution.py
@@ -16,6 +16,9 @@
 CHANNELS = 64
 OUT = 512
 ROWS = TAPS * SUB
+PARTS = 3
+PIECE = 9 * SUB
+DEPTH = SUB * PIECE
 MESH = pl.DeviceIdType.MESH
 
 
@@ -41,6 +44,7 @@
     z_out,
     z_in,
     g_buf,
+    m_buf,
     b_buf,
     rot_buf,
     fin_buf,
@@ -126,13 +130,6 @@
         jnp.logical_and(tm > 0, me < CHIPS - 1),
     )
 
-    pl.semaphore_wait(barrier, SLABS + CHIPS + PANELS - 3)
-    for i in range(3):
-
-        @pl.when(sends[i])
-        def _():
-            halo(i).start()
-
     @pl.loop(0, BLOCKS)
     def _(b):
         block = grad_ref[order_ref[b // 4], lax.rem(b // 2, 2), lax.rem(b, 2)]
@@ -140,6 +137,13 @@
         p_buf[rows, :] = lax.dot_general(
             block, ob_ref[...], (((0,), (0,)), ((), ())), preferred_element_type=jnp.float32
         ).astype(jnp.bfloat16)
+
+    pl.semaphore_wait(barrier, SLABS + CHIPS + PANELS - 3)
+    for i in range(3):
+
+        @pl.when(sends[i])
+        def _():
+            halo(i).start()
 
     def half(which):
         return pl.ds(pl.multiple_of(which * 2 * LANES, 2 * LANES), 2 * LANES)
@@ -189,132 +193,130 @@
     for cb in range(SUB):
         first = cb * ROWS // LANES * LANES
         last = min(first + 3 * LANES, bt_ref.shape[1])
-        row = lax.broadcasted_iota(jnp.int32, (last - first, ROWS), 0)
-        col = lax.broadcasted_iota(jnp.int32, (last - first, ROWS), 1)
-        wanted = cb * ROWS - first + lax.rem(col, SUB) * TAPS + col // SUB
-        pick = jnp.where(row == wanted, 1.0, 0.0).astype(jnp.bfloat16)
-        b_buf[cb] = jnp.dot(
-            bt_ref[:, first:last], pick, preferred_element_type=jnp.float32
-        ).astype(jnp.bfloat16)
+        row = lax.broadcasted_iota(jnp.int32, (ROWS, last - first), 0)
+        col = lax.broadcasted_iota(jnp.int32, (ROWS, last - first), 1)
+        wanted = cb * ROWS - first + lax.rem(row, SUB) * TAPS + row // SUB
+        pick = jnp.where(col == wanted, 1.0, 0.0).astype(jnp.bfloat16)
+        moved = lax.dot_general(
+            pick,
+            bt_ref[:, first:last],
+            (((1,), (1,)), ((), ())),
+            preferred_element_type=jnp.float32,
+        )
+        for p in range(PARTS):
+            m_buf[p, cb * PIECE : (cb + 1) * PIECE, :] = moved[p * PIECE : (p + 1) * PIECE]
+    for p in range(PARTS):
+        b_buf[p] = m_buf[p].T.astype(jnp.bfloat16)
     rot_buf[...] = jnp.zeros_like(rot_buf)
 
-    @pl.when(receives[0])
-    def _():
-        halo(0).wait_recv()
-
-    for i in (3, 4):
-
-        @pl.when(sends[i])
-        def _():
-            halo(i).start()
-
-    for i in (3, 4):
-
-        @pl.when(receives[i])
-        def _():
-            halo(i).wait_recv()
-
-    taps_of(1)
-    taps_of(0)
-
-    def plane_copy(d):
-        return pltpu.make_async_remote_copy(
-            src_ref=s_buf.at[d],
-            dst_ref=r_buf.at[d],
-            send_sem=s_send.at[d],
-            recv_sem=s_recv.at[d],
+    def plane_copy(p, d):
+        return pltpu.make_async_remote_copy(
+            src_ref=s_buf.at[p, d],
+            dst_ref=r_buf.at[p, d],
+            send_sem=s_send.at[p, d],
+            recv_sem=s_recv.at[p, d],
             device_id={"height": lax.rem(me + d, CHIPS)},
             device_id_type=MESH,
         )
 
-    def chunk(d):
+    def chunk(p, d):
         chip = lax.rem(me + d, CHIPS)
         low = chip // SUB
+        taps = pl.ds(9 * p, 9)
         rows = pl.ds(pl.multiple_of(lax.rem(chip, SUB) * SUB, SUB), SUB)
-        own = t_buf[:, rows, pl.ds(pl.multiple_of((2 * core + low) * LANES, LANES), LANES)]
-        other = c_buf[:, rows, pl.ds(pl.multiple_of(low * LANES, LANES), LANES)]
-        return (own + other).reshape(ROWS, LANES)
-
-    for dt in (2, 1, 0):
-        pair_copy(dt).wait_recv()
-
-    @pl.loop(1, CHIPS)
-    def _(d):
-        s_buf[d] = chunk(d).astype(jnp.bfloat16)
-        plane_copy(d).start()
-
-    acc[...] = chunk(0)
-
-    @pl.loop(1, CHIPS)
-    def _(d):
-        plane_copy(d).wait_recv()
-        acc[...] += r_buf[d].astype(jnp.float32)
-
-    z_out[...] = acc[...].astype(jnp.bfloat16)
-    z_copy = pltpu.make_async_remote_copy(
-        src_ref=z_out,
-        dst_ref=z_in,
-        send_sem=z_send,
-        recv_sem=z_recv,
-        device_id={"tm": far},
-        device_id_type=MESH,
-    )
-    z_copy.start()
-    z_copy.wait_recv()
-
-    def place(which, d):
+        own = t_buf[taps, rows, pl.ds(pl.multiple_of((2 * core + low) * LANES, LANES), LANES)]
+        other = c_buf[taps, rows, pl.ds(pl.multiple_of(low * LANES, LANES), LANES)]
+        return (own + other).reshape(PIECE, LANES)
+
+    def plane_start(p):
+        pair_copy(p).wait_recv()
+
+        @pl.loop(1, CHIPS)
+        def _(d):
+            s_buf[p, d] = chunk(p, d).astype(jnp.bfloat16)
+            plane_copy(p, d).start()
+
+        acc[p] = chunk(p, 0)
+
+    def z_copy(p):
+        return pltpu.make_async_remote_copy(
+            src_ref=z_out.at[p],
+            dst_ref=z_in.at[p],
+            send_sem=z_send.at[p],
+            recv_sem=z_recv.at[p],
+            device_id={"tm": far},
+            device_id_type=MESH,
+        )
+
+    def plane_finish(p):
+        @pl.loop(1, CHIPS)
+        def _(d):
+            plane_copy(p, d).wait_recv()
+            acc[p] += r_buf[p, d].astype(jnp.float32)
+
+        z_out[p] = acc[p].astype(jnp.bfloat16)
+        z_copy(p).start()
+
+    def place(d):
         owner = lax.rem(me - d + CHIPS, CHIPS)
-        return 2 * which + owner // SUB, lax.rem(owner, SUB)
-
-    def gather_copy(d):
-        kb, cb = place(core, 0)
-        return pltpu.make_async_remote_copy(
-            src_ref=g_buf.at[kb, cb],
-            dst_ref=g_buf.at[kb, cb],
-            send_sem=g_send.at[d],
-            recv_sem=g_recv.at[d],
+        return 2 * core + owner // SUB, lax.rem(owner, SUB)
+
+    def gather_copy(p, d):
+        kb, cb = place(0)
+        return pltpu.make_async_remote_copy(
+            src_ref=g_buf.at[p, kb, cb],
+            dst_ref=g_buf.at[p, kb, cb],
+            send_sem=g_send.at[p, d],
+            recv_sem=g_recv.at[p, d],
             device_id={"height": lax.rem(me + d, CHIPS)},
             device_id_type=MESH,
         )
 
-    def hand_copy(d):
-        kb, cb = place(core, d)
-        return pltpu.make_async_remote_copy(
-            src_ref=g_buf.at[kb, cb],
-            dst_ref=g_buf.at[kb, cb],
-            send_sem=f_send.at[d],
-            recv_sem=f_recv.at[d],
+    def hand_copy(p, d):
+        kb, cb = place(d)
+        return pltpu.make_async_remote_copy(
+            src_ref=g_buf.at[p, kb, cb],
+            dst_ref=g_buf.at[p, kb, cb],
+            send_sem=f_send.at[p, d],
+            recv_sem=f_recv.at[p, d],
             device_id={"tm": mate},
             device_id_type=MESH,
         )
 
-    def rotate(which, d):
-        kb, cb = place(which, d)
-        rot_buf[kb] += jnp.dot(b_buf[cb], g_buf[kb, cb], preferred_element_type=jnp.float32)
-
-    kb0, cb0 = place(core, 0)
-    g_buf[kb0, cb0] = (acc[...] + z_in[...].astype(jnp.float32)).astype(jnp.bfloat16)
-
-    @pl.loop(1, CHIPS)
-    def _(d):
-        gather_copy(d).start()
-
-    hand_copy(0).start()
-    rotate(core, 0)
-
-    @pl.loop(1, CHIPS)
-    def _(d):
-        gather_copy(d).wait_recv()
-        hand_copy(d).start()
-        rotate(core, d)
-
-    @pl.loop(0, CHIPS)
-    def _(d):
-        hand_copy(d).wait_recv()
-        rotate(1 - core, d)
-
-    for kb in range(4):
-        fin_buf[2 * kb : 2 * kb + 2] = rot_buf[kb].T.reshape(2, CHANNELS, ROWS)
+    def z_finish(p):
+        z_copy(p).wait_recv()
+        kb, cb = place(0)
+        g_buf[p, kb, cb] = (acc[p] + z_in[p].astype(jnp.float32)).astype(jnp.bfloat16)
+
+        @pl.loop(1, CHIPS)
+        def _(d):
+            gather_copy(p, d).start()
+
+        hand_copy(p, 0).start()
+
+    def rotate(which, p):
+        sides = [
+            g_buf[p, 2 * which + i].astype(jnp.float32).reshape(DEPTH, LANES).astype(jnp.bfloat16)
+            for i in range(2)
+        ]
+        rot_buf[which] += jnp.dot(
+            b_buf[p], jnp.concatenate(sides, axis=1), preferred_element_type=jnp.float32
+        )
+
+    def gather_finish(p):
+        @pl.loop(1, CHIPS)
+        def _(d):
+            gather_copy(p, d).wait_recv()
+            hand_copy(p, d).start()
+
+        rotate(core, p)
+
+    def hand_finish(p):
+        @pl.loop(0, CHIPS)
+        def _(d):
+            hand_copy(p, d).wait_recv()
+
+        rotate(1 - core, p)
 
     def panel_copy(d):
         return pltpu.make_async_remote_copy(
@@ -326,10 +328,55 @@
             device_id_type=MESH,
         )
 
-    @pl.loop(1, PANELS)
-    def _(d):
-        q_buf[d] = fin_buf[lax.rem(panel + d, PANELS)].astype(jnp.bfloat16)
-        panel_copy(d).start()
+    def panel_start(which):
+        fin_buf[pl.ds(4 * which, 4)] = rot_buf[which].T.reshape(4, CHANNELS, ROWS)
+
+        @pl.loop(0, 4)
+        def _(i):
+            target = 4 * which + i
+
+            @pl.when(target != panel)
+            def _():
+                d = lax.rem(target - panel + PANELS, PANELS)
+                q_buf[d] = fin_buf[target].astype(jnp.bfloat16)
+                panel_copy(d).start()
+
+    @pl.when(receives[0])
+    def _():
+        halo(0).wait_recv()
+
+    for i in (3, 4):
+
+        @pl.when(sends[i])
+        def _():
+            halo(i).start()
+
+    plane_start(2)
+
+    for i in (3, 4):
+
+        @pl.when(receives[i])
+        def _():
+            halo(i).wait_recv()
+
+    taps_of(1)
+    plane_finish(2)
+    taps_of(0)
+    plane_start(1)
+    plane_start(0)
+    plane_finish(1)
+    z_finish(2)
+    plane_finish(0)
+    z_finish(1)
+    gather_finish(2)
+    hand_finish(2)
+    z_finish(0)
+    gather_finish(1)
+    hand_finish(1)
+    gather_finish(0)
+    panel_start(core)
+    hand_finish(0)
+    panel_start(1 - core)
 
     out_ref[...] = fin_buf[panel]
 
@@ -346,16 +393,16 @@
         def _():
             halo(i).wait_send()
 
-    for dt in range(3):
-        pair_copy(dt).wait_send()
-    z_copy.wait_send()
-    hand_copy(0).wait_send()
-
-    @pl.loop(1, CHIPS)
-    def _(d):
-        plane_copy(d).wait_send()
-        gather_copy(d).wait_send()
-        hand_copy(d).wait_send()
+    for p in range(PARTS):
+        pair_copy(p).wait_send()
+        z_copy(p).wait_send()
+        hand_copy(p, 0).wait_send()
+
+        @pl.loop(1, CHIPS)
+        def _(d):
+            plane_copy(p, d).wait_send()
+            gather_copy(p, d).wait_send()
+            hand_copy(p, d).wait_send()
 
     @pl.loop(1, PANELS)
     def _(d):
@@ -378,14 +425,15 @@
             pltpu.VMEM((positions, OUT), bf16),
             pltpu.VMEM((TAPS, CHANNELS, OUT), f32),
             pltpu.VMEM((TAPS, CHANNELS, OUT // 2), f32),
-            pltpu.VMEM((CHIPS, ROWS, LANES), bf16),
-            pltpu.VMEM((CHIPS, ROWS, LANES), bf16),
-            pltpu.VMEM((ROWS, LANES), f32),
-            pltpu.VMEM((ROWS, LANES), bf16),
-            pltpu.VMEM((ROWS, LANES), bf16),
-            pltpu.VMEM((4, SUB, ROWS, LANES), bf16),
-            pltpu.VMEM((SUB, ROWS, ROWS), bf16),
-            pltpu.VMEM((4, ROWS, LANES), f32),
+            pltpu.VMEM((PARTS, CHIPS, PIECE, LANES), bf16),
+            pltpu.VMEM((PARTS, CHIPS, PIECE, LANES), bf16),
+            pltpu.VMEM((PARTS, PIECE, LANES), f32),
+            pltpu.VMEM((PARTS, PIECE, LANES), bf16),
+            pltpu.VMEM((PARTS, PIECE, LANES), bf16),
+            pltpu.VMEM((PARTS, 4, SUB, PIECE, LANES), bf16),
+            pltpu.VMEM((PARTS, DEPTH, ROWS), f32),
+            pltpu.VMEM((PARTS, ROWS, DEPTH), bf16),
+            pltpu.VMEM((2, ROWS, 2 * LANES), f32),
             pltpu.VMEM((PANELS, CHANNELS, ROWS), f32),
             pltpu.VMEM((PANELS, CHANNELS, ROWS), bf16),
             pltpu.VMEM((PANELS, CHANNELS, ROWS), bf16),
@@ -393,14 +441,14 @@
             dma((5,)),
             dma((3,)),
             dma((3,)),
-            dma((CHIPS,)),
-            dma((CHIPS,)),
-            dma(()),
-            dma(()),
-            dma((CHIPS,)),
-            dma((CHIPS,)),
-            dma((CHIPS,)),
-            dma((CHIPS,)),
+            dma((PARTS, CHIPS)),
+            dma((PARTS, CHIPS)),
+            dma((PARTS,)),
+            dma((PARTS,)),
+            dma((PARTS, CHIPS)),
+            dma((PARTS, CHIPS)),
+            dma((PARTS, CHIPS)),
+            dma((PARTS, CHIPS)),
             dma((PANELS,)),
             dma((PANELS,)),
         ],

time: 92.5 us -> 80.8 us (0.87); the launches traced: 90.7 us -> 80.7 us
  Pallas kernels: 89.2 us -> 79.2 us
    pallas_call x1, Pallas kernels: 89.2 us -> 79.2 us  [body(): pl.pallas_call(kernel, out_shape=jax.ShapeDtypeStruct(eigenvalues.shape,...]
where the time goes in v3:
time: 80.8 us; the launch traced here: 80.7 us
  Pallas kernels  79.2 us (98%)
  local copies, waits for them, and re-layouts  1.47 us (2%)
    pallas_call x1, Pallas kernels, body(): pl.pallas_call(kernel, out_shape=jax.ShapeDtypeStruct(eigenvalues.shape,...  79.2 us

profile of v3, /device:TPU:1, one launch (start us, length us, event | category | flops | bytes accessed | tf_op | source)
XLA Modules:
  0.0 80.7 jit_solution(16687106436179134813)
XLA Ops:
  0.0 79.2 %shard_map.64 = f32[64,216]{1,0:T(8,128)} custom-call(s32[6]{0:T(128)} %order_ref.1, bf16[6,2,2,64,128]{4,3,2,1,0:T(8,128)(2,1)} %act_ref.1, bf16[6,2,2,512,128]{4,3,2,1,0:T(8,128)(2,1)} %grad_ref.1, bf16[512,512]{1,0:T(8,128)(2,1)} %ob_ref.1, bf16[216,1728]{1,0:T(8,128)(2,1)} %bitcast.1, f32[64,216]{1,0:T(8,128)} %eig_ref.1), custom_call_target="tpu_custom_call" | custom-call | tf_op jit(solution)/shard_map/pallas_call | solution.py:417
  79.2 1.5 %copy.8 = f32[64,216]{1,0:T(8,128)} copy(f32[64,216]{1,0:T(8,128)} %shard_map.64) | data formatting | bytes 110592

commit v4 on v3

--- a/solution.py
+++ b/solution.py
@@ -27,12 +27,18 @@
 
 def kernel(
     order_ref,
+    act_in,
+    grad_in,
+    ob_in,
+    bt_in,
+    eig_in,
+    out_ref,
     act_ref,
     grad_ref,
     ob_ref,
     bt_ref,
     eig_ref,
-    out_ref,
+    in_sem,
     e_buf,
     w_buf,
     p_buf,
@@ -83,6 +89,22 @@
                 barrier, inc=1, device_id={axis: lax.rem(mine + d, count)}, device_id_type=MESH
             )
 
+    loads = [
+        pltpu.make_async_copy(source, target, in_sem.at[i])
+        for i, (source, target) in enumerate(
+            (
+                (act_in, act_ref),
+                (ob_in, ob_ref),
+                (grad_in, grad_ref),
+                (bt_in, bt_ref),
+                (eig_in, eig_ref),
+            )
+        )
+    ]
+    for load in loads:
+        load.start()
+    loads[0].wait()
+
     for n in range(FORGET):
         e_buf[n, 2:4, 1:3] = act_ref[order_ref[n]]
 
@@ -130,6 +152,16 @@
         jnp.logical_and(tm > 0, me < CHIPS - 1),
     )
 
+    pl.semaphore_wait(barrier, SLABS + CHIPS + PANELS - 3)
+    for i in range(3):
+
+        @pl.when(sends[i])
+        def _():
+            halo(i).start()
+
+    loads[1].wait()
+    loads[2].wait()
+
     @pl.loop(0, BLOCKS)
     def _(b):
         block = grad_ref[order_ref[b // 4], lax.rem(b // 2, 2), lax.rem(b, 2)]
@@ -138,13 +170,6 @@
             block, ob_ref[...], (((0,), (0,)), ((), ())), preferred_element_type=jnp.float32
         ).astype(jnp.bfloat16)
 
-    pl.semaphore_wait(barrier, SLABS + CHIPS + PANELS - 3)
-    for i in range(3):
-
-        @pl.when(sends[i])
-        def _():
-            halo(i).start()
-
     def half(which):
         return pl.ds(pl.multiple_of(which * 2 * LANES, 2 * LANES), 2 * LANES)
 
@@ -160,22 +185,29 @@
 
     column = lax.broadcasted_iota(jnp.int32, (CHANNELS, LANES), 1)
 
-    def taps_of(dt):
-        @pl.loop(0, BLOCKS)
-        def _(b):
-            n, f, r = b // 4, lax.rem(b // 2, 2), lax.rem(b, 2)
-            lanes = pl.ds(pl.multiple_of(b * LANES, LANES), LANES)
-            for dh in range(3):
-                tile = e_buf[n, f + dt, r + dh]
+    def windows(e):
+        @pl.loop(0, FORGET)
+        def _(n):
+            for q in range(4):
+                tile = e_buf[n, e, q]
                 wide = tile.astype(jnp.float32)
                 left = jnp.where(column == 0, 0.0, pltpu.roll(wide, 1, 1)).astype(jnp.bfloat16)
                 right = jnp.where(column == LANES - 1, 0.0, pltpu.roll(wide, LANES - 1, 1)).astype(
                     jnp.bfloat16
                 )
-                for dw, shifted in enumerate((left, tile, right)):
-                    at = (dt * 9 + dh * 3 + dw) * CHANNELS
-                    w_buf[at : at + CHANNELS, lanes] = shifted
-
+                for f in range(2):
+                    for r in range(2):
+                        dt, dh = e - f, q - r
+                        if not (0 <= dt < 3 and 0 <= dh < 3):
+                            continue
+                        lanes = pl.ds(
+                            pl.multiple_of(n * 4 * LANES, LANES) + (f * 2 + r) * LANES, LANES
+                        )
+                        for dw, shifted in enumerate((left, tile, right)):
+                            at = (dt * 9 + dh * 3 + dw) * CHANNELS
+                            w_buf[at : at + CHANNELS, lanes] = shifted
+
+    def taps_of(dt):
         at = dt * 9 * CHANNELS
         t_buf[dt * 9 : dt * 9 + 9] = jnp.dot(
             w_buf[at : at + 9 * CHANNELS, :], p_buf[...], preferred_element_type=jnp.float32
@@ -188,7 +220,170 @@
         def _():
             halo(i).wait_recv()
 
+    windows(2)
+    windows(3)
     taps_of(2)
+
+    def plane_copy(p, d):
+        return pltpu.make_async_remote_copy(
+            src_ref=s_buf.at[p, d],
+            dst_ref=r_buf.at[p, d],
+            send_sem=s_send.at[p, d],
+            recv_sem=s_recv.at[p, d],
+            device_id={"height": lax.rem(me + d, CHIPS)},
+            device_id_type=MESH,
+        )
+
+    def chunk(p, d):
+        chip = lax.rem(me + d, CHIPS)
+        low = chip // SUB
+        taps = pl.ds(9 * p, 9)
+        rows = pl.ds(pl.multiple_of(lax.rem(chip, SUB) * SUB, SUB), SUB)
+        own = t_buf[taps, rows, pl.ds(pl.multiple_of((2 * core + low) * LANES, LANES), LANES)]
+        other = c_buf[taps, rows, pl.ds(pl.multiple_of(low * LANES, LANES), LANES)]
+        return (own + other).reshape(PIECE, LANES)
+
+    def plane_start(p):
+        pair_copy(p).wait_recv()
+
+        @pl.loop(1, CHIPS)
+        def _(d):
+            s_buf[p, d] = chunk(p, d).astype(jnp.bfloat16)
+            plane_copy(p, d).start()
+
+        acc[p] = chunk(p, 0)
+
+    def z_copy(p):
+        return pltpu.make_async_remote_copy(
+            src_ref=z_out.at[p],
+            dst_ref=z_in.at[p],
+            send_sem=z_send.at[p],
+            recv_sem=z_recv.at[p],
+            device_id={"tm": far},
+            device_id_type=MESH,
+        )
+
+    def plane_finish(p):
+        @pl.loop(1, CHIPS)
+        def _(d):
+            plane_copy(p, d).wait_recv()
+            acc[p] += r_buf[p, d].astype(jnp.float32)
+
+        z_out[p] = acc[p].astype(jnp.bfloat16)
+        z_copy(p).start()
+
+    def place(d):
+        owner = lax.rem(me - d + CHIPS, CHIPS)
+        return 2 * core + owner // SUB, lax.rem(owner, SUB)
+
+    def gather_copy(p, d):
+        kb, cb = place(0)
+        return pltpu.make_async_remote_copy(
+            src_ref=g_buf.at[p, kb, cb],
+            dst_ref=g_buf.at[p, kb, cb],
+            send_sem=g_send.at[p, d],
+            recv_sem=g_recv.at[p, d],
+            device_id={"height": lax.rem(me + d, CHIPS)},
+            device_id_type=MESH,
+        )
+
+    def hand_copy(p, d):
+        kb, cb = place(d)
+        return pltpu.make_async_remote_copy(
+            src_ref=g_buf.at[p, kb, cb],
+            dst_ref=g_buf.at[p, kb, cb],
+            send_sem=f_send.at[p, d],
+            recv_sem=f_recv.at[p, d],
+            device_id={"tm": mate},
+            device_id_type=MESH,
+        )
+
+    def z_finish(p):
+        z_copy(p).wait_recv()
+        kb, cb = place(0)
+        g_buf[p, kb, cb] = (acc[p] + z_in[p].astype(jnp.float32)).astype(jnp.bfloat16)
+
+        @pl.loop(1, CHIPS)
+        def _(d):
+            gather_copy(p, d).start()
+
+        hand_copy(p, 0).start()
+
+    def rotate(which, p):
+        sides = [
+            g_buf[p, 2 * which + i].astype(jnp.float32).reshape(DEPTH, LANES).astype(jnp.bfloat16)
+            for i in range(2)
+        ]
+        rot_buf[which] += jnp.dot(
+            b_buf[p], jnp.concatenate(sides, axis=1), preferred_element_type=jnp.float32
+        )
+
+    def gather_finish(p):
+        @pl.loop(1, CHIPS)
+        def _(d):
+            gather_copy(p, d).wait_recv()
+            hand_copy(p, d).start()
+
+        rotate(core, p)
+
+    def hand_finish(p):
+        @pl.loop(0, CHIPS)
+        def _(d):
+            hand_copy(p, d).wait_recv()
+
+        rotate(1 - core, p)
+
+    def panel_copy(d):
+        return pltpu.make_async_remote_copy(
+            src_ref=q_buf.at[d],
+            dst_ref=y_buf.at[d],
+            send_sem=q_send.at[d],
+            recv_sem=q_recv.at[d],
+            device_id={"panel": lax.rem(panel + d, PANELS)},
+            device_id_type=MESH,
+        )
+
+    def panel_start(which):
+        fin_buf[pl.ds(4 * which, 4)] = rot_buf[which].T.reshape(4, CHANNELS, ROWS)
+
+        @pl.loop(0, 4)
+        def _(i):
+            target = 4 * which + i
+
+            @pl.when(target != panel)
+            def _():
+                d = lax.rem(target - panel + PANELS, PANELS)
+                q_buf[d] = fin_buf[target].astype(jnp.bfloat16)
+                panel_copy(d).start()
+
+    @pl.when(receives[0])
+    def _():
+        halo(0).wait_recv()
+
+    for i in (3, 4):
+
+        @pl.when(sends[i])
+        def _():
+            halo(i).start()
+
+    for i in (3, 4):
+
+        @pl.when(receives[i])
+        def _():
+            halo(i).wait_recv()
+
+    windows(1)
+    plane_start(2)
+    taps_of(1)
+    windows(0)
+    plane_start(1)
+    taps_of(0)
+    plane_finish(2)
+    plane_start(0)
+    plane_finish(1)
+
+    loads[3].wait()
+    loads[4].wait()
 
     for cb in range(SUB):
         first = cb * ROWS // LANES * LANES
@@ -209,162 +404,6 @@
         b_buf[p] = m_buf[p].T.astype(jnp.bfloat16)
     rot_buf[...] = jnp.zeros_like(rot_buf)
 
-    def plane_copy(p, d):
-        return pltpu.make_async_remote_copy(
-            src_ref=s_buf.at[p, d],
-            dst_ref=r_buf.at[p, d],
-            send_sem=s_send.at[p, d],
-            recv_sem=s_recv.at[p, d],
-            device_id={"height": lax.rem(me + d, CHIPS)},
-            device_id_type=MESH,
-        )
-
-    def chunk(p, d):
-        chip = lax.rem(me + d, CHIPS)
-        low = chip // SUB
-        taps = pl.ds(9 * p, 9)
-        rows = pl.ds(pl.multiple_of(lax.rem(chip, SUB) * SUB, SUB), SUB)
-        own = t_buf[taps, rows, pl.ds(pl.multiple_of((2 * core + low) * LANES, LANES), LANES)]
-        other = c_buf[taps, rows, pl.ds(pl.multiple_of(low * LANES, LANES), LANES)]
-        return (own + other).reshape(PIECE, LANES)
-
-    def plane_start(p):
-        pair_copy(p).wait_recv()
-
-        @pl.loop(1, CHIPS)
-        def _(d):
-            s_buf[p, d] = chunk(p, d).astype(jnp.bfloat16)
-            plane_copy(p, d).start()
-
-        acc[p] = chunk(p, 0)
-
-    def z_copy(p):
-        return pltpu.make_async_remote_copy(
-            src_ref=z_out.at[p],
-            dst_ref=z_in.at[p],
-            send_sem=z_send.at[p],
-            recv_sem=z_recv.at[p],
-            device_id={"tm": far},
-            device_id_type=MESH,
-        )
-
-    def plane_finish(p):
-        @pl.loop(1, CHIPS)
-        def _(d):
-            plane_copy(p, d).wait_recv()
-            acc[p] += r_buf[p, d].astype(jnp.float32)
-
-        z_out[p] = acc[p].astype(jnp.bfloat16)
-        z_copy(p).start()
-
-    def place(d):
-        owner = lax.rem(me - d + CHIPS, CHIPS)
-        return 2 * core + owner // SUB, lax.rem(owner, SUB)
-
-    def gather_copy(p, d):
-        kb, cb = place(0)
-        return pltpu.make_async_remote_copy(
-            src_ref=g_buf.at[p, kb, cb],
-            dst_ref=g_buf.at[p, kb, cb],
-            send_sem=g_send.at[p, d],
-            recv_sem=g_recv.at[p, d],
-            device_id={"height": lax.rem(me + d, CHIPS)},
-            device_id_type=MESH,
-        )
-
-    def hand_copy(p, d):
-        kb, cb = place(d)
-        return pltpu.make_async_remote_copy(
-            src_ref=g_buf.at[p, kb, cb],
-            dst_ref=g_buf.at[p, kb, cb],
-            send_sem=f_send.at[p, d],
-            recv_sem=f_recv.at[p, d],
-            device_id={"tm": mate},
-            device_id_type=MESH,
-        )
-
-    def z_finish(p):
-        z_copy(p).wait_recv()
-        kb, cb = place(0)
-        g_buf[p, kb, cb] = (acc[p] + z_in[p].astype(jnp.float32)).astype(jnp.bfloat16)
-
-        @pl.loop(1, CHIPS)
-        def _(d):
-            gather_copy(p, d).start()
-
-        hand_copy(p, 0).start()
-
-    def rotate(which, p):
-        sides = [
-            g_buf[p, 2 * which + i].astype(jnp.float32).reshape(DEPTH, LANES).astype(jnp.bfloat16)
-            for i in range(2)
-        ]
-        rot_buf[which] += jnp.dot(
-            b_buf[p], jnp.concatenate(sides, axis=1), preferred_element_type=jnp.float32
-        )
-
-    def gather_finish(p):
-        @pl.loop(1, CHIPS)
-        def _(d):
-            gather_copy(p, d).wait_recv()
-            hand_copy(p, d).start()
-
-        rotate(core, p)
-
-    def hand_finish(p):
-        @pl.loop(0, CHIPS)
-        def _(d):
-            hand_copy(p, d).wait_recv()
-
-        rotate(1 - core, p)
-
-    def panel_copy(d):
-        return pltpu.make_async_remote_copy(
-            src_ref=q_buf.at[d],
-            dst_ref=y_buf.at[d],
-            send_sem=q_send.at[d],
-            recv_sem=q_recv.at[d],
-            device_id={"panel": lax.rem(panel + d, PANELS)},
-            device_id_type=MESH,
-        )
-
-    def panel_start(which):
-        fin_buf[pl.ds(4 * which, 4)] = rot_buf[which].T.reshape(4, CHANNELS, ROWS)
-
-        @pl.loop(0, 4)
-        def _(i):
-            target = 4 * which + i
-
-            @pl.when(target != panel)
-            def _():
-                d = lax.rem(target - panel + PANELS, PANELS)
-                q_buf[d] = fin_buf[target].astype(jnp.bfloat16)
-                panel_copy(d).start()
-
-    @pl.when(receives[0])
-    def _():
-        halo(0).wait_recv()
-
-    for i in (3, 4):
-
-        @pl.when(sends[i])
-        def _():
-            halo(i).start()
-
-    plane_start(2)
-
-    for i in (3, 4):
-
-        @pl.when(receives[i])
-        def _():
-            halo(i).wait_recv()
-
-    taps_of(1)
-    plane_finish(2)
-    taps_of(0)
-    plane_start(1)
-    plane_start(0)
-    plane_finish(1)
     z_finish(2)
     plane_finish(0)
     z_finish(1)
@@ -417,9 +456,15 @@
     return pl.pallas_call(
         kernel,
         out_shape=jax.ShapeDtypeStruct(eigenvalues.shape, f32),
-        in_specs=[pl.BlockSpec(memory_space=pltpu.SMEM)] + [vmem] * 5,
+        in_specs=[pl.BlockSpec(memory_space=pltpu.SMEM)] + [pl.BlockSpec(memory_space=pl.ANY)] * 5,
         out_specs=vmem,
         scratch_shapes=[
+            pltpu.VMEM(activations.shape, bf16),
+            pltpu.VMEM(out_grad.shape, bf16),
+            pltpu.VMEM(out_basis.shape, bf16),
+            pltpu.VMEM(in_basis.shape[::-1], bf16),
+            pltpu.VMEM(eigenvalues.shape, f32),
+            dma((5,)),
             pltpu.VMEM((FORGET, 4, 4, CHANNELS, LANES), bf16),
             pltpu.VMEM((TAPS * CHANNELS, positions), bf16),
             pltpu.VMEM((positions, OUT), bf16),

time: 80.8 us -> 77.8 us (0.963)
  Pallas kernels: 79.2 us -> 76.1 us
    pallas_call x1, Pallas kernels: 79.2 us -> 76.1 us  [body(): pl.pallas_call(kernel, out_shape=jax.ShapeDtypeStruct(eigenvalues.shape,...]
where the time goes in v4:
time: 77.8 us; the launch traced here: 77.6 us
  Pallas kernels  76.1 us (98%)
  local copies, waits for them, and re-layouts  1.47 us (2%)
    pallas_call x1, Pallas kernels, body(): pl.pallas_call(kernel, out_shape=jax.ShapeDtypeStruct(eigenvalues.shape,...  76.1 us

profile of v4, /device:TPU:1, one launch (start us, length us, event | category | flops | bytes accessed | tf_op | source)
XLA Modules:
  0.0 77.6 jit_solution(14801407420792043327)
XLA Ops:
  0.0 76.1 %shard_map.64 = f32[64,216]{1,0:T(8,128)} custom-call(s32[6]{0:T(128)} %order_ref.1, bf16[6,2,2,64,128]{4,3,2,1,0:T(8,128)(2,1)} %act_in.1, bf16[6,2,2,512,128]{4,3,2,1,0:T(8,128)(2,1)} %grad_in.1, bf16[512,512]{1,0:T(8,128)(2,1)} %ob_in.1, bf16[216,1728]{1,0:T(8,128)(2,1)} %bitcast.1, f32[64,216]{1,0:T(8,128)} %eig_in.1), custom_call_target="tpu_custom_call" | custom-call | tf_op jit(solution)/shard_map/pallas_call | solution.py:456
  76.1 1.5 %copy.8 = f32[64,216]{1,0:T(8,128)} copy(f32[64,216]{1,0:T(8,128)} %shard_map.64) | data formatting | bytes 110592

commit v5 on v4

--- a/solution.py
+++ b/solution.py
@@ -404,8 +404,8 @@
         b_buf[p] = m_buf[p].T.astype(jnp.bfloat16)
     rot_buf[...] = jnp.zeros_like(rot_buf)
 
+    plane_finish(0)
     z_finish(2)
-    plane_finish(0)
     z_finish(1)
     gather_finish(2)
     hand_finish(2)

time: 77.8 us -> 78.9 us (1.014)
  Pallas kernels: 76.1 us -> 77.2 us
    pallas_call x1, Pallas kernels: 76.1 us -> 77.2 us  [body(): pl.pallas_call(kernel, out_shape=jax.ShapeDtypeStruct(eigenvalues.shape,...]
where the time goes in v5:
time: 78.9 us; the launch traced here: 78.7 us
  Pallas kernels  77.2 us (98%)
  local copies, waits for them, and re-layouts  1.47 us (2%)
    pallas_call x1, Pallas kernels, body(): pl.pallas_call(kernel, out_shape=jax.ShapeDtypeStruct(eigenvalues.shape,...  77.2 us

profile of v5, /device:TPU:1, one launch (start us, length us, event | category | flops | bytes accessed | tf_op | source)
XLA Modules:
  0.0 78.7 jit_solution(9610826405783691438)
XLA Ops:
  0.0 77.2 %shard_map.64 = f32[64,216]{1,0:T(8,128)} custom-call(s32[6]{0:T(128)} %order_ref.1, bf16[6,2,2,64,128]{4,3,2,1,0:T(8,128)(2,1)} %act_in.1, bf16[6,2,2,512,128]{4,3,2,1,0:T(8,128)(2,1)} %grad_in.1, bf16[512,512]{1,0:T(8,128)(2,1)} %ob_in.1, bf16[216,1728]{1,0:T(8,128)(2,1)} %bitcast.1, f32[64,216]{1,0:T(8,128)} %eig_in.1), custom_call_target="tpu_custom_call" | custom-call | tf_op jit(solution)/shard_map/pallas_call | solution.py:456
  77.2 1.5 %copy.8 = f32[64,216]{1,0:T(8,128)} copy(f32[64,216]{1,0:T(8,128)} %shard_map.64) | data formatting | bytes 110592
